TPU v7x, 512 devices: a whole 4x4x16 slice. The times are simulated.
512 devices in a mesh: cuts: 128 (over z, x, core), stem: 4 (over y).
Axes of the slice: x: 4, y: 4, z: 16, core: 2. Of those that a mesh axis runs over, the one named last changes fastest.
Arguments:
- stem_tensor: bfloat16 [8, 64, 1024], P('stem'), may hold values from -6 to 6
- mid_tensors: bfloat16 [8192, 512, 128], P(('cuts', 'stem')), may hold values from -0.1875 to 0.1875
- right_tensors: bfloat16 [8, 8192, 64, 128], P(None, ('cuts', 'stem')), may hold values from -0.001953125 to 0.001953125
Outputs:
- amplitudes: float32 [8192], P('cuts')
All inputs are finite; a program needn't handle non-finite values.
Results may differ from a plain program's by a relative error of at most 0.0029.
Values may be sent and summed in bfloat16 or wider, within the bound.
A program may use at most 64 MiB of HBM per device.

v0:
```python
import jax
import jax.numpy as jnp
from jax import lax
from jax.sharding import PartitionSpec as P


def widen(tensor):
    half_width = tensor.shape[-1] // 2
    real_part = tensor[..., :half_width]
    imag_part = tensor[..., half_width:]
    upper_rows = jnp.concatenate([real_part, imag_part], axis=-1)
    lower_rows = jnp.concatenate([-imag_part, real_part], axis=-1)
    return jnp.concatenate([upper_rows, lower_rows], axis=-2)


def on_device(stem_tensor, mid_tensors, right_tensors):
    local_blocks, rows_a, width = stem_tensor.shape
    cols_b = right_tensors.shape[-1]
    widened = jnp.moveaxis(widen(mid_tensors), 0, 1).reshape(width, -1)
    fragment = lax.all_gather(stem_tensor, "stem", axis=0, tiled=True)
    flattened = fragment.reshape(-1, width)
    product = jnp.dot(flattened, widened, preferred_element_type=jnp.float32)
    first_step = product.astype(jnp.bfloat16).reshape(fragment.shape[0], rows_a, -1)
    right_wide = widen(right_tensors).reshape(first_step.shape[0], -1, cols_b)
    partial_sum = jnp.einsum(
        "iaq,iqb->ab", first_step, right_wide, preferred_element_type=jnp.float32
    ).reshape(-1)
    summed = lax.psum(partial_sum, ("cuts", "stem"))
    portion = partial_sum.shape[0] // lax.axis_size("cuts")
    return lax.dynamic_slice_in_dim(summed, lax.axis_index("cuts") * portion, portion)


def solution(mesh):
    return jax.shard_map(
        on_device,
        mesh=mesh,
        in_specs=(
            P("stem", None, None),
            P(("cuts", "stem"), None, None),
            P(None, ("cuts", "stem"), None, None),
        ),
        out_specs=P("cuts"),
        check_vma=False,
    )
```

profile of v0, /device:TPU:1, one launch (start us, length us, event | category | flops | bytes accessed | tf_op | source)
XLA Modules:
  0.0 163.8 jit_solution(10493150595197969950)
XLA Ops:
  6.5 0.0 all-gather.2.cloned.1.call-start
  6.5 0.7 all-gather.2.cloned.1.call-update
  7.3 2.9 %copy.9 = bf16[16,512,128]{1,2,0:T(8,128)(2,1)S(1)} copy(bf16[16,512,128]{2,1,0:T(8,128)(2,1)} %param.4) | data formatting | bytes 4194304 | tf_op args[1]
  10.1 0.1 slice_negate_fusion.1
  10.3 0.0 copy-start.1
  10.3 2.2 %maximum_maximum_fusion = bf16[16,1024,128]{1,2,0:T(8,128)(2,1)} fusion(bf16[16,512,64]{1,2,0:T(8,128)(2,1)S(1)} %get-tuple-element.8, bf16[16,512,64]{1,2,0:T(8,128)(2,1)S(1)} %get-tuple-element.7, bf16[16,512,128]{1,2,0:T(8,128)(2,1)S(1)} %copy.9), kind=kLoop, calls=%fused_computation | loop fusion | flops 12582912 | bytes 8388608 | tf_op jit(solution)/shard_map/concatenate | solution.py:13
  12.5 0.1 copy-done.1
  12.6 0.9 slice_negate_fusion
  13.5 3.5 %maximum_maximum_fusion.1 = bf16[8,16,128,128]{3,2,1,0:T(8,128)(2,1)} fusion(bf16[8,16,64,64]{3,2,1,0:T(8,128)(2,1)S(1)} %get-tuple-element.6, bf16[8,16,64,64]{3,2,1,0:T(8,128)(2,1)S(1)} %get-tuple-element.5, bf16[8,16,64,128]{3,2,1,0:T(8,128)(2,1)S(1)} %copy-done.1), kind=kLoop, calls=%fused_computation.1 | loop fusion | flops 12582912 | bytes 8388608 | tf_op jit(solution)/shard_map/concatenate | solution.py:13
  17.0 28.6 %all-gather.2.cloned.1.call-done = bf16[8,64,1024]{2,1,0:T(8,128)(2,1)} async-done(((bf16[2,64,1024]{2,1,0:T(8,128)(2,1)}), bf16[8,64,1024]{2,1,0:T(8,128)(2,1)}) %all-gather.2.cloned.1.call-update) | async-done | bytes 1048592 | tf_op jit(solution)/shard_map/all_gather | solution.py:20
  45.6 0.0 copy-start
  45.6 5.0 %convolution_convert_fusion = bf16[2048,512]{0,1:T(8,128)(2,1)S(1)} fusion(bf16[1024,2048]{0,1:T(8,128)(2,1)} %bitcast.18, bf16[512,1024]{1,0:T(8,128)(2,1)} %bitcast.19), kind=kOutput, calls=%fused_computation.2 | convolution fusion | flops 2148532224 | bytes 7340032 | tf_op jit(solution)/shard_map/dot_general | solution.py:22
  50.6 0.0 copy-done
  50.6 0.9 convolution_bitcast_fusion
  51.4 105.0 %psum.7 = f32[8192]{0:T(1024)S(1)} all-reduce(f32[8192]{0:T(1024)S(1)} %convolution_bitcast_fusion), channel_id=1, replica_groups=mesh['cuts'=128,'stem'=4] {'cuts','stem'}, use_global_device_ids=true, to_apply=%region_0.0 | all-reduce | flops 8192 | bytes 65536 | tf_op jit(solution)/shard_map/psum | solution.py:28
  156.4 0.6 dynamic_slice.3
Async XLA Ops:
  6.5 39.0 %all-gather.2.cloned.1.call-start = ((), (), s32[]{:S(2)}) async-start(), calls=%async_computation | async-start | bytes 1310720 | tf_op jit(solution)/shard_map/all_gather | solution.py:20
  10.3 2.3 %copy-start.1 = (bf16[8,16,64,128]{3,2,1,0:T(8,128)(2,1)S(1)}, bf16[8,16,64,128]{3,2,1,0:T(8,128)(2,1)}, u32[]{:S(2)}) copy-start(bf16[8,16,64,128]{3,2,1,0:T(8,128)(2,1)} %param.5) | copy-start | bytes 6291460
  45.6 5.0 %copy-start = (bf16[8,16,128,128]{3,2,1,0:T(8,128)(2,1)S(1)}, bf16[8,16,128,128]{3,2,1,0:T(8,128)(2,1)}, u32[]{:S(2)}) copy-start(bf16[8,16,128,128]{3,2,1,0:T(8,128)(2,1)} %maximum_maximum_fusion.1) | copy-start | bytes 12582916
Sparse Core Ops, SparseCore 0:
  9.5 36.0 all-gather.1
where the time goes:
time: 164 us
  blocking collectives  105 us (64%)
  waiting for transfers between devices  29.3 us (18%)
  between operations  13.4 us (8%)
  other arithmetic  6.78 us (4%)
  matrix products  5.86 us (4%)
  local copies, waits for them, and re-layouts  3.52 us (2%)
    psum x1, blocking collectives, on_device(): summed = lax.psum(partial_sum, ('cuts', 'stem'))  105 us
    all_gather x1, waiting for transfers between devices, on_device(): fragment = lax.all_gather(stem_tensor, 'stem', axis=0, tiled=True)  28.6 us
    concatenate x2, other arithmetic, widen(): return jnp.concatenate([upper_rows, lower_rows], axis=-2)  5.77 us
    dot_general x1, matrix products, on_device(): product = jnp.dot(flattened, widened, preferred_element_type=jnp.float32)  5.01 us
  transfers between devices with their start and end apart: 1, of which 1 were waited for; matrix products, arithmetic and copies ran while one was open for 6% of the time, Pallas kernels for 0%

commit v1 on v0

v1 whole, which is shorter than its diff:
```python
import functools

import jax
import jax.numpy as jnp
from jax import lax
from jax.experimental import pallas as pl
from jax.experimental.pallas import tpu as pltpu
from jax.sharding import PartitionSpec as P

MESH = pl.DeviceIdType.MESH
NX = 4
NCORE = 2


def kernel(
    nz, ny,
    stem_hbm, mid_hbm, right_hbm, out_ref,
    stem_v, mid_v, right_v, rhs_v, lhs_v, acc_v, send1, recv1, send2, recv2,
    stem_sem, mid_sem, right_sem, gs_send, gs_recv, r_send, r_recv,
):
    cut, y = lax.axis_index("cuts"), lax.axis_index("stem")
    core = lax.rem(cut, NCORE)
    x = lax.rem(cut // NCORE, NX)
    z = cut // (NCORE * NX)
    plane = NX * NCORE * ny
    part = y * NCORE + core
    parts = NCORE * ny
    per = nz // parts
    place = x * parts + part

    def at(z_, x_, part_):
        return ((z_ * NX + x_) * NCORE + lax.rem(part_, NCORE), part_ // NCORE)

    barrier = pltpu.get_barrier_semaphore()

    @pl.loop(1, plane)
    def _(d):
        peer = lax.rem(place + d, plane)
        pl.semaphore_signal(
            barrier, inc=1, device_id=at(z, peer // parts, lax.rem(peer, parts)), device_id_type=MESH
        )

    owner = z // per
    in_own = owner == part

    @pl.loop(0, nz)
    def _(d):
        z_ = lax.rem(z + d, nz)

        @pl.when(jnp.logical_not(jnp.logical_and(d == 0, in_own)))
        def _():
            pl.semaphore_signal(barrier, inc=1, device_id=at(z_, x, owner), device_id_type=MESH)

    blocks = stem_hbm.shape[0]
    copies = [pltpu.make_async_copy(mid_hbm, mid_v, mid_sem)]
    copies.append(pltpu.make_async_copy(stem_hbm, stem_v.at[pl.ds(y * blocks, blocks)], stem_sem))
    copies.append(pltpu.make_async_copy(right_hbm, right_v, right_sem))
    for copy in copies:
        copy.start()

    pl.semaphore_wait(barrier, plane - 1 + per * parts - in_own.astype(jnp.int32))

    rows = stem_hbm.shape[1]
    half = rows // 2
    up, down = lax.rem(y + 1, ny), lax.rem(y + ny - 1, ny)
    far = lax.rem(y + 2, ny)
    other = cut + 1 - 2 * core

    def piece(y_, h):
        return stem_v.at[y_ * blocks + core, pl.ds(h * half, half)]

    def push(n, src, dst, device):
        return pltpu.make_async_remote_copy(
            src_ref=src, dst_ref=dst, send_sem=gs_send.at[n], recv_sem=gs_recv.at[n],
            device_id=device, device_id_type=MESH,
        )

    mine = [stem_hbm.at[core, pl.ds(h * half, half)] for h in (0, 1)]
    first = [
        push(0, mine[0], piece(y, 0), (cut, up)),
        push(1, mine[1], piece(y, 1), (cut, down)),
        push(2, mine[1], piece(y, 1), (cut, up)),
        push(3, mine[0], piece(y, 0), (cut, down)),
    ]
    for copy in first:
        copy.start()
    arrives = [(down, 0), (up, 1), (down, 1), (up, 0), (far, 0), (far, 1)]
    onward = [push(4, piece(down, 0), piece(down, 0), (cut, up)), push(5, piece(up, 1), piece(up, 1), (cut, down))]
    shared = [push(6 + n, piece(*arrives[n]), piece(*arrives[n]), (other, y)) for n in range(6)]

    copies[0].wait()
    depth, width = mid_hbm.shape[1:]
    r = width // 2
    for p in range(mid_hbm.shape[0] // 2):
        a, b = mid_v[2 * p], mid_v[2 * p + 1]
        rhs_v[0:depth, p * width:(p + 1) * width] = jnp.concatenate([a[:, :r], b[:, :r]], axis=1)
        rhs_v[depth:, p * width:(p + 1) * width] = jnp.concatenate([a[:, r:], b[:, r:]], axis=1)

    acc_v[...] = jnp.zeros_like(acc_v)
    tile = 256

    def contract(y_):
        for b in range(blocks):
            s = stem_v[y_ * blocks + b]
            re, im = s[:, :depth], s[:, depth:]
            base = b * 2 * rows
            lhs_v[base:base + rows, :depth] = re
            lhs_v[base:base + rows, depth:] = -im
            lhs_v[base + rows:base + 2 * rows, :depth] = im
            lhs_v[base + rows:base + 2 * rows, depth:] = re
        for n in range(rhs_v.shape[1] // tile):
            f = jnp.dot(
                lhs_v[...], rhs_v[:, n * tile:(n + 1) * tile], preferred_element_type=jnp.float32
            ).astype(jnp.bfloat16)
            for b in range(blocks):
                acc_v[...] += jnp.dot(
                    f[b * 2 * rows:(b + 1) * 2 * rows],
                    right_v[y_ * blocks + b, n * tile:(n + 1) * tile, :],
                    preferred_element_type=jnp.float32,
                )

    copies[1].wait()
    copies[2].wait()
    contract(y)
    for n in (0, 1):
        first[n].wait_recv()
        onward[n].start()
        shared[n].start()
    for n in (2, 3):
        first[n].wait_recv()
        shared[n].start()
    for n in (0, 2):
        shared[n].wait_recv()
    contract(down)
    for n in (0, 1):
        onward[n].wait_recv()
        shared[4 + n].start()
    for n in (1, 3):
        shared[n].wait_recv()
    contract(up)
    for n in (4, 5):
        shared[n].wait_recv()
    contract(far)

    top, bottom = acc_v[0:rows], acc_v[rows:]
    turned = pltpu.roll(bottom, r, axis=1)
    lane = lax.broadcasted_iota(jnp.int32, turned.shape, 1)
    total = top + jnp.where(lane < r, -turned, turned)
    for part_ in range(parts):
        for x_ in range(NX):
            for k in range(per):
                row = (part_ * per + k) * NX + x_
                send1[part_ * NX + x_, k:k + 1, :] = total[row:row + 1]

    @pl.loop(1, plane)
    def _(d):
        peer = lax.rem(place + d, plane)
        x_, part_ = peer // parts, lax.rem(peer, parts)
        pltpu.make_async_remote_copy(
            src_ref=send1.at[part_ * NX + x_], dst_ref=recv1.at[place],
            send_sem=r_send.at[0], recv_sem=r_recv.at[0],
            device_id=at(z, x_, part_), device_id_type=MESH,
        ).start()

    recv1[place] = send1[part * NX + x]
    all1 = pltpu.make_async_remote_copy(
        src_ref=send1.at[pl.ds(0, plane - 1)], dst_ref=recv1.at[pl.ds(0, plane - 1)],
        send_sem=r_send.at[0], recv_sem=r_recv.at[0], device_id=(cut, y), device_id_type=MESH,
    )
    all1.wait_recv()
    sums = recv1[0]
    for n in range(1, plane):
        sums = sums + recv1[n]
    for k in range(per):
        send2[k] = sums[k:k + 1]

    def target(t):
        k, part_ = t // parts, lax.rem(lax.rem(t, parts) + part, parts)
        z_ = part * per + k
        return k, z_, part_

    @pl.loop(0, per * parts)
    def _(t):
        k, z_, part_ = target(t)
        own = jnp.logical_and(z_ == z, part_ == part)

        @pl.when(jnp.logical_not(own))
        def _():
            pltpu.make_async_remote_copy(
                src_ref=send2.at[k], dst_ref=recv2.at[z],
                send_sem=r_send.at[1], recv_sem=r_recv.at[1],
                device_id=at(z_, x, part_), device_id_type=MESH,
            ).start()

        @pl.when(own)
        def _():
            recv2[z] = send2[k]

    def all2(n):
        return pltpu.make_async_remote_copy(
            src_ref=recv2.at[pl.ds(0, n)], dst_ref=recv2.at[pl.ds(0, n)],
            send_sem=r_send.at[1], recv_sem=r_recv.at[1], device_id=(cut, y), device_id_type=MESH,
        )

    @pl.when(in_own)
    def _():
        all2(nz - 1).wait_recv()

    @pl.when(jnp.logical_not(in_own))
    def _():
        all2(nz).wait_recv()

    result = recv2[0]
    for n in range(1, nz):
        result = result + recv2[n]
    out_ref[...] = jnp.where(core == 0, result[:, :r], result[:, r:])

    for copy in first + onward + shared:
        copy.wait_send()
    all1.wait_send()

    @pl.when(in_own)
    def _():
        all2(nz - 1).wait_send()

    @pl.when(jnp.logical_not(in_own))
    def _():
        all2(nz).wait_send()


def on_device(nz, ny, stem_tensor, mid_tensors, right_tensors):
    blocks, rows, width = stem_tensor.shape
    terms, pairs, r, cols = right_tensors.shape
    depth = mid_tensors.shape[1]
    plane = NX * NCORE * ny
    per = nz // (NCORE * ny)
    anywhere = pl.BlockSpec(memory_space=pl.ANY)
    out = pl.pallas_call(
        functools.partial(kernel, nz, ny),
        out_shape=jax.ShapeDtypeStruct((1, cols // 2), jnp.float32),
        in_specs=[anywhere] * 3,
        out_specs=pl.BlockSpec(memory_space=pltpu.VMEM),
        scratch_shapes=[
            pltpu.VMEM((terms, rows, width), jnp.bfloat16),
            pltpu.VMEM(mid_tensors.shape, jnp.bfloat16),
            pltpu.VMEM((terms, pairs * r, cols), jnp.bfloat16),
            pltpu.VMEM((2 * depth, pairs * r), jnp.bfloat16),
            pltpu.VMEM((blocks * 2 * rows, width), jnp.bfloat16),
            pltpu.VMEM((2 * rows, cols), jnp.float32),
            pltpu.VMEM((plane, per, cols), jnp.float32),
            pltpu.VMEM((plane, per, cols), jnp.float32),
            pltpu.VMEM((per, 1, cols), jnp.float32),
            pltpu.VMEM((nz, 1, cols), jnp.float32),
            pltpu.SemaphoreType.DMA,
            pltpu.SemaphoreType.DMA,
            pltpu.SemaphoreType.DMA,
            pltpu.SemaphoreType.DMA((12,)),
            pltpu.SemaphoreType.DMA((12,)),
            pltpu.SemaphoreType.DMA((2,)),
            pltpu.SemaphoreType.DMA((2,)),
        ],
        compiler_params=pltpu.CompilerParams(
            collective_id=0, has_side_effects=True, vmem_limit_bytes=60 * 2**20
        ),
    )(stem_tensor, mid_tensors, right_tensors.reshape(terms, pairs * r, cols))
    return out.reshape(-1)


def solution(mesh):
    return jax.shard_map(
        functools.partial(on_device, mesh.shape["cuts"] // (NX * NCORE), mesh.shape["stem"]),
        mesh=mesh,
        in_specs=(
            P("stem", None, None),
            P(("cuts", "stem"), None, None),
            P(None, ("cuts", "stem"), None, None),
        ),
        out_specs=P("cuts"),
        check_vma=False,
    )
```

time: 164 us -> 43.7 us (0.27)
  blocking collectives: 105 us -> 0 us
  Pallas kernels: 0 us -> 42.3 us
  waiting for transfers between devices: 29.3 us -> 0 us
  between operations: 13.4 us -> 0.01 us
  other arithmetic: 6.78 us -> 0 us
  matrix products: 5.86 us -> 0 us
  local copies, waits for them, and re-layouts: 3.52 us -> 1.19 us
    psum x1 -> x0, blocking collectives: 105 us -> none  [on_device(): summed = lax.psum(partial_sum, ('cuts', 'stem'))]
    pallas_call x0 -> x1, Pallas kernels: none -> 42.3 us  [on_device(): pl.pallas_call(functools.partial(kernel, nz, ny), out_shape=jax.ShapeDtyp...]
    all_gather x1 -> x0, waiting for transfers between devices: 28.6 us -> none  [on_device(): fragment = lax.all_gather(stem_tensor, 'stem', axis=0, tiled=True)]
    dot_general x2 -> x0, matrix products: 5.86 us -> none  [the longest x1 5.01 us: on_device(): product = jnp.dot(flattened, widened, preferred_element_type=jnp.float32)]
    concatenate x2 -> x0, other arithmetic: 5.77 us -> none  [widen(): return jnp.concatenate([upper_rows, lower_rows], axis=-2)]
    unnamed x5 -> x1, local copies, waits for them, and re-layouts: 2.94 us -> 1.19 us
  transfers between devices with their start and end apart: 1 -> 0, of which waited for: 1 -> 0; matrix products, arithmetic and copies ran while one was open for 6% -> 0% of each run, Pallas kernels for 0% -> 0%
where the time goes in v1:
time: 43.7 us; the launch traced here: 43.5 us
  Pallas kernels  42.3 us (97%)
  local copies, waits for them, and re-layouts  1.19 us (3%)
    pallas_call x1, Pallas kernels, on_device(): pl.pallas_call(functools.partial(kernel, nz, ny), out_shape=jax.ShapeDtyp...  42.3 us
    unnamed x1, local copies, waits for them, and re-layouts  1.19 us

profile of v1, /device:TPU:1, one launch (start us, length us, event | category | flops | bytes accessed | tf_op | source)
XLA Modules:
  0.0 43.5 jit_solution(12791146459587334831)
XLA Ops:
  0.0 42.3 %shard_map.37 = f32[1,64]{1,0:T(1,128)} custom-call(bf16[2,64,1024]{2,1,0:T(8,128)(2,1)} %stem_hbm.1, bf16[16,512,128]{2,1,0:T(8,128)(2,1)} %mid_hbm.1, bf16[8,1024,128]{2,1,0:T(8,128)(2,1)} %bitcast.2), custom_call_target="tpu_custom_call" | custom-call | tf_op jit(solution)/shard_map/pallas_call | solution.py:238
  42.4 1.2 %copy.5 = f32[64]{0:T(128)} copy(f32[64]{0:T(128)} %bitcast.3) | data formatting | bytes 512

commit v2 on v1

v2 whole, which is shorter than its diff:
```python
import functools

import jax
import jax.numpy as jnp
from jax import lax
from jax.experimental import pallas as pl
from jax.experimental.pallas import tpu as pltpu
from jax.sharding import PartitionSpec as P

MESH = pl.DeviceIdType.MESH
NX = 4
NCORE = 2


def tree_sum(values):
    while len(values) > 1:
        odd = values[len(values) // 2 * 2:]
        values = [a + b for a, b in zip(values[::2], values[1::2])] + odd
    return values[0]


def kernel(
    nz, ny,
    stem_hbm, mid_hbm, right_hbm, out_ref,
    stem_v, mid_v, right_v, rhs_v, lhs_v, mix_v, acc_v, send1, recv1, send2, recv2,
    stem_sem, mid_sem, right_sem, gs_send, gs_recv, r_send, r_recv,
):
    cut, y = lax.axis_index("cuts"), lax.axis_index("stem")
    core = lax.rem(cut, NCORE)
    x = lax.rem(lax.div(cut, NCORE), NX)
    z = lax.div(cut, NCORE * NX)
    plane = NX * NCORE * ny
    parts = NCORE * ny
    part = y * NCORE + core
    per = nz // parts
    xs = [lax.rem(x + d, NX) for d in range(NX)]
    ys = [lax.rem(y + d, ny) for d in range(ny)]
    cores = [core, 1 - core]

    def hops(d, n):
        return min(d, n - d)

    def signal(device):
        pl.semaphore_signal(barrier, inc=1, device_id=device, device_id_type=MESH)

    def at(z_, x_, core_):
        return (z_ * NX + x_) * NCORE + core_

    barrier = pltpu.get_barrier_semaphore()
    for d in range(1, ny):
        signal((cut, ys[d]))
    for d in range(NX):
        for c in range(NCORE):
            if d or c:
                signal((at(z, xs[d], cores[c]), y))
    for d in range(1, nz):
        signal((at(lax.rem(z + d, nz), x, core), y))

    blocks = stem_hbm.shape[0]
    load_stem = pltpu.make_async_copy(stem_hbm, stem_v.at[pl.ds(y * blocks, blocks)], stem_sem)
    load_mid = pltpu.make_async_copy(mid_hbm, mid_v, mid_sem)
    load_right = pltpu.make_async_copy(right_hbm, right_v, right_sem)
    load_stem.start()
    load_mid.start()
    load_right.start()
    pl.semaphore_wait(barrier, (ny - 1) + (NX * NCORE - 1) + (nz - 1))

    rows = stem_hbm.shape[1]
    half = rows // 2
    up, far, down = ys[1], ys[2], ys[3]
    other = at(z, x, cores[1])

    def piece(y_, h):
        return stem_v.at[y_ * blocks + core, pl.ds(h * half, half)]

    def push(n, src, dst, device):
        return pltpu.make_async_remote_copy(
            src_ref=src, dst_ref=dst, send_sem=gs_send.at[n], recv_sem=gs_recv.at[n],
            device_id=device, device_id_type=MESH,
        )

    mine = [stem_hbm.at[core, pl.ds(h * half, half)] for h in (0, 1)]
    first = [
        push(0, mine[0], piece(y, 0), (cut, up)),
        push(1, mine[1], piece(y, 1), (cut, down)),
        push(2, mine[1], piece(y, 1), (cut, up)),
        push(3, mine[0], piece(y, 0), (cut, down)),
    ]
    for copy in first:
        copy.start()
    arrives = [(down, 0), (up, 1), (down, 1), (up, 0), (far, 0), (far, 1)]
    onward = [push(4, piece(down, 0), piece(down, 0), (cut, up)), push(5, piece(up, 1), piece(up, 1), (cut, down))]
    shared = [push(6 + n, piece(*arrives[n]), piece(*arrives[n]), (other, y)) for n in range(6)]

    depth, width = mid_hbm.shape[1:]
    r = width // 2
    load_mid.wait()
    for p in range(mid_hbm.shape[0] // 2):
        a, b = mid_v[2 * p], mid_v[2 * p + 1]
        rhs_v[0:depth, p * width:(p + 1) * width] = jnp.concatenate([a[:, :r], b[:, :r]], axis=1)
        rhs_v[depth:, p * width:(p + 1) * width] = jnp.concatenate([a[:, r:], b[:, r:]], axis=1)

    tile = 256

    def contract(slot, y_, core_, start=False):
        s = stem_v[y_ * blocks + core_]
        re, im = s[:, :depth], s[:, depth:]
        lhs_v[slot, :rows, :depth] = re
        lhs_v[slot, :rows, depth:] = -im
        lhs_v[slot, rows:, :depth] = im
        lhs_v[slot, rows:, depth:] = re
        for n in range(rhs_v.shape[1] // tile):
            mix_v[slot, :, n * tile:(n + 1) * tile] = jnp.dot(
                lhs_v[slot], rhs_v[:, n * tile:(n + 1) * tile], preferred_element_type=jnp.float32
            ).astype(jnp.bfloat16)
        update = jnp.dot(mix_v[slot], right_v[y_ * blocks + core_], preferred_element_type=jnp.float32)
        acc_v[...] = update if start else acc_v[...] + update

    load_stem.wait()
    load_right.wait()
    contract(0, y, cores[0], start=True)
    contract(1, y, cores[1])
    for n in (0, 1):
        first[n].wait_recv()
        onward[n].start()
        shared[n].start()
    for n in (2, 3):
        first[n].wait_recv()
        shared[n].start()
    contract(0, down, cores[0])
    contract(1, up, cores[0])
    for n in (0, 2):
        shared[n].wait_recv()
    for n in (0, 1):
        onward[n].wait_recv()
        shared[4 + n].start()
    contract(0, down, cores[1])
    contract(1, far, cores[0])
    for n in (1, 3):
        shared[n].wait_recv()
    contract(0, up, cores[1])
    for n in (4, 5):
        shared[n].wait_recv()
    contract(1, far, cores[1])

    top, bottom = acc_v[0:rows], acc_v[rows:]
    turned = pltpu.roll(bottom, r, axis=1)
    lane = lax.broadcasted_iota(jnp.int32, turned.shape, 1)
    total = top + jnp.where(lane < r, -turned, turned)
    for part_ in range(parts):
        for x_ in range(NX):
            for k in range(per):
                row = (part_ * per + k) * NX + x_
                send1[part_ * NX + x_, k:k + 1, :] = total[row:row + 1]

    place = x * parts + part
    peers = [(dx, dy, dc) for dx in range(NX) for dy in range(ny) for dc in range(NCORE)]
    peers.sort(key=lambda d: -(hops(d[0], NX) + hops(d[1], ny) + 0.5 * d[2]))
    for dx, dy, dc in peers:
        part_ = ys[dy] * NCORE + cores[dc]
        if dx or dy or dc:
            pltpu.make_async_remote_copy(
                src_ref=send1.at[part_ * NX + xs[dx]], dst_ref=recv1.at[place],
                send_sem=r_send.at[0], recv_sem=r_recv.at[0],
                device_id=(at(z, xs[dx], cores[dc]), ys[dy]), device_id_type=MESH,
            ).start()
    recv1[place] = send1[part * NX + x]
    all1 = pltpu.make_async_remote_copy(
        src_ref=send1.at[pl.ds(0, plane - 1)], dst_ref=recv1.at[pl.ds(0, plane - 1)],
        send_sem=r_send.at[0], recv_sem=r_recv.at[0], device_id=(cut, y), device_id_type=MESH,
    )
    all1.wait_recv()
    sums = tree_sum([recv1[n] for n in range(plane)])
    for k in range(per):
        send2[k] = sums[k:k + 1]

    def deliver(k, device):
        pltpu.make_async_remote_copy(
            src_ref=send2.at[k], dst_ref=recv2.at[z],
            send_sem=r_send.at[1], recv_sem=r_recv.at[1], device_id=device, device_id_type=MESH,
        ).start()

    for dy in sorted(range(ny), key=lambda d: hops(d, ny)):
        for dc in range(NCORE):
            for k in range(per):
                z_ = part * per + k
                device = (at(z_, x, cores[dc]), ys[dy])
                if dy or dc:
                    deliver(k, device)
                else:
                    pl.when(z_ != z)(functools.partial(deliver, k, device))

                    @pl.when(z_ == z)
                    def _():
                        recv2[z] = send2[k]

    in_own = lax.div(z, per) == part

    def all2(n):
        return pltpu.make_async_remote_copy(
            src_ref=recv2.at[pl.ds(0, n)], dst_ref=recv2.at[pl.ds(0, n)],
            send_sem=r_send.at[1], recv_sem=r_recv.at[1], device_id=(cut, y), device_id_type=MESH,
        )

    @pl.when(in_own)
    def _():
        all2(nz - 1).wait_recv()

    @pl.when(jnp.logical_not(in_own))
    def _():
        all2(nz).wait_recv()

    out_ref[...] = tree_sum([recv2[n] for n in range(nz)])

    for copy in first + onward + shared:
        copy.wait_send()
    all1.wait_send()

    @pl.when(in_own)
    def _():
        all2(nz - 1).wait_send()

    @pl.when(jnp.logical_not(in_own))
    def _():
        all2(nz).wait_send()


def on_device(nz, ny, stem_tensor, mid_tensors, right_tensors):
    blocks, rows, width = stem_tensor.shape
    terms, pairs, r, cols = right_tensors.shape
    depth = mid_tensors.shape[1]
    plane = NX * NCORE * ny
    per = nz // (NCORE * ny)
    anywhere = pl.BlockSpec(memory_space=pl.ANY)
    out = pl.pallas_call(
        functools.partial(kernel, nz, ny),
        out_shape=jax.ShapeDtypeStruct((1, cols), jnp.float32),
        in_specs=[anywhere] * 3,
        out_specs=pl.BlockSpec(memory_space=pltpu.VMEM),
        scratch_shapes=[
            pltpu.VMEM((terms, rows, width), jnp.bfloat16),
            pltpu.VMEM(mid_tensors.shape, jnp.bfloat16),
            pltpu.VMEM((terms, pairs * r, cols), jnp.bfloat16),
            pltpu.VMEM((2 * depth, pairs * r), jnp.bfloat16),
            pltpu.VMEM((2, 2 * rows, width), jnp.bfloat16),
            pltpu.VMEM((2, 2 * rows, pairs * r), jnp.bfloat16),
            pltpu.VMEM((2 * rows, cols), jnp.float32),
            pltpu.VMEM((plane, per, cols), jnp.float32),
            pltpu.VMEM((plane, per, cols), jnp.float32),
            pltpu.VMEM((per, 1, cols), jnp.float32),
            pltpu.VMEM((nz, 1, cols), jnp.float32),
            pltpu.SemaphoreType.DMA,
            pltpu.SemaphoreType.DMA,
            pltpu.SemaphoreType.DMA,
            pltpu.SemaphoreType.DMA((12,)),
            pltpu.SemaphoreType.DMA((12,)),
            pltpu.SemaphoreType.DMA((2,)),
            pltpu.SemaphoreType.DMA((2,)),
        ],
        compiler_params=pltpu.CompilerParams(
            collective_id=0, has_side_effects=True, vmem_limit_bytes=60 * 2**20
        ),
    )(stem_tensor, mid_tensors, right_tensors.reshape(terms, pairs * r, cols))
    portion = cols // NCORE
    start = lax.rem(lax.axis_index("cuts"), NCORE) * portion
    return lax.dynamic_slice_in_dim(out.reshape(-1), start, portion)


def solution(mesh):
    return jax.shard_map(
        functools.partial(on_device, mesh.shape["cuts"] // (NX * NCORE), mesh.shape["stem"]),
        mesh=mesh,
        in_specs=(
            P("stem", None, None),
            P(("cuts", "stem"), None, None),
            P(None, ("cuts", "stem"), None, None),
        ),
        out_specs=P("cuts"),
        check_vma=False,
    )
```

time: 43.7 us -> 40.7 us (0.931)
  Pallas kernels: 42.3 us -> 39.3 us
    pallas_call x1, Pallas kernels: 42.3 us -> 39.3 us  [on_device(): pl.pallas_call(functools.partial(kernel, nz, ny), out_shape=jax.ShapeDtyp...]
    dynamic_slice x0 -> x1, local copies, waits for them, and re-layouts: none -> 1.27 us  [on_device(): return lax.dynamic_slice_in_dim(out.reshape(-1), start, portion)]
    unnamed x1 -> x0, local copies, waits for them, and re-layouts: 1.19 us -> none
where the time goes in v2:
time: 40.7 us; the launch traced here: 40.5 us
  Pallas kernels  39.3 us (97%)
  local copies, waits for them, and re-layouts  1.27 us (3%)
    pallas_call x1, Pallas kernels, on_device(): pl.pallas_call(functools.partial(kernel, nz, ny), out_shape=jax.ShapeDtyp...  39.3 us
    dynamic_slice x1, local copies, waits for them, and re-layouts, on_device(): return lax.dynamic_slice_in_dim(out.reshape(-1), start, portion)  1.27 us

profile of v2, /device:TPU:1, one launch (start us, length us, event | category | flops | bytes accessed | tf_op | source)
XLA Modules:
  0.0 40.5 jit_solution(10750757915224457693)
XLA Ops:
  0.0 39.3 %shard_map.37 = f32[1,128]{1,0:T(1,128)} custom-call(bf16[2,64,1024]{2,1,0:T(8,128)(2,1)} %stem_hbm.1, bf16[16,512,128]{2,1,0:T(8,128)(2,1)} %mid_hbm.1, bf16[8,1024,128]{2,1,0:T(8,128)(2,1)} %bitcast.3), custom_call_target="tpu_custom_call" | custom-call | tf_op jit(solution)/shard_map/pallas_call | solution.py:235
  39.3 1.3 %dynamic-slice_bitcast_fusion = f32[64]{0:T(128)} fusion(f32[1,128]{1,0:T(1,128)} %shard_map.37, s32[]{:T(128)S(6)} %select_n.3), kind=kLoop, calls=%fused_computation | loop fusion | bytes 516 | tf_op jit(solution)/shard_map/dynamic_slice | solution.py:266

commit v3 on v2

--- a/solution.py
+++ b/solution.py
@@ -80,17 +80,23 @@
         )
 
     mine = [stem_hbm.at[core, pl.ds(h * half, half)] for h in (0, 1)]
-    first = [
+    arriving = [
         push(0, mine[0], piece(y, 0), (cut, up)),
         push(1, mine[1], piece(y, 1), (cut, down)),
         push(2, mine[1], piece(y, 1), (cut, up)),
         push(3, mine[0], piece(y, 0), (cut, down)),
+        push(4, mine[0], piece(y, 0), (cut, far)),
+        push(5, mine[1], piece(y, 1), (cut, far)),
     ]
-    for copy in first:
+    for copy in arriving:
         copy.start()
-    arrives = [(down, 0), (up, 1), (down, 1), (up, 0), (far, 0), (far, 1)]
-    onward = [push(4, piece(down, 0), piece(down, 0), (cut, up)), push(5, piece(up, 1), piece(up, 1), (cut, down))]
-    shared = [push(6 + n, piece(*arrives[n]), piece(*arrives[n]), (other, y)) for n in range(6)]
+    arrived = [piece(down, 0), piece(up, 1), piece(down, 1), piece(up, 0), piece(far, 0), piece(far, 1)]
+    shared = [push(6 + n, arrived[n], arrived[n], (other, y)) for n in range(6)]
+
+    def share(*which):
+        for n in which:
+            arriving[n].wait_recv()
+            shared[n].start()
 
     depth, width = mid_hbm.shape[1:]
     r = width // 2
@@ -120,21 +126,13 @@
     load_right.wait()
     contract(0, y, cores[0], start=True)
     contract(1, y, cores[1])
-    for n in (0, 1):
-        first[n].wait_recv()
-        onward[n].start()
-        shared[n].start()
-    for n in (2, 3):
-        first[n].wait_recv()
-        shared[n].start()
+    share(0, 1, 2, 3)
     contract(0, down, cores[0])
     contract(1, up, cores[0])
     for n in (0, 2):
         shared[n].wait_recv()
-    for n in (0, 1):
-        onward[n].wait_recv()
-        shared[4 + n].start()
     contract(0, down, cores[1])
+    share(4, 5)
     contract(1, far, cores[0])
     for n in (1, 3):
         shared[n].wait_recv()
@@ -154,16 +152,17 @@
                 send1[part_ * NX + x_, k:k + 1, :] = total[row:row + 1]
 
     place = x * parts + part
-    peers = [(dx, dy, dc) for dx in range(NX) for dy in range(ny) for dc in range(NCORE)]
-    peers.sort(key=lambda d: -(hops(d[0], NX) + hops(d[1], ny) + 0.5 * d[2]))
-    for dx, dy, dc in peers:
-        part_ = ys[dy] * NCORE + cores[dc]
-        if dx or dy or dc:
-            pltpu.make_async_remote_copy(
-                src_ref=send1.at[part_ * NX + xs[dx]], dst_ref=recv1.at[place],
-                send_sem=r_send.at[0], recv_sem=r_recv.at[0],
-                device_id=(at(z, xs[dx], cores[dc]), ys[dy]), device_id_type=MESH,
-            ).start()
+
+    def send(part_, x_):
+        pltpu.make_async_remote_copy(
+            src_ref=send1.at[part_ * NX + x_], dst_ref=recv1.at[place],
+            send_sem=r_send.at[0], recv_sem=r_recv.at[0],
+            device_id=(at(z, x_, part_ % NCORE), part_ // NCORE), device_id_type=MESH,
+        ).start()
+
+    for part_ in range(parts):
+        for x_ in range(NX):
+            pl.when(place != x_ * parts + part_)(functools.partial(send, part_, x_))
     recv1[place] = send1[part * NX + x]
     all1 = pltpu.make_async_remote_copy(
         src_ref=send1.at[pl.ds(0, plane - 1)], dst_ref=recv1.at[pl.ds(0, plane - 1)],
@@ -180,9 +179,9 @@
             send_sem=r_send.at[1], recv_sem=r_recv.at[1], device_id=device, device_id_type=MESH,
         ).start()
 
-    for dy in sorted(range(ny), key=lambda d: hops(d, ny)):
-        for dc in range(NCORE):
-            for k in range(per):
+    for k in range(per):
+        for dy in sorted(range(ny), key=lambda d: hops(d, ny)):
+            for dc in reversed(range(NCORE)):
                 z_ = part * per + k
                 device = (at(z_, x, cores[dc]), ys[dy])
                 if dy or dc:
@@ -212,7 +211,7 @@
 
     out_ref[...] = tree_sum([recv2[n] for n in range(nz)])
 
-    for copy in first + onward + shared:
+    for copy in arriving + shared:
         copy.wait_send()
     all1.wait_send()
 
@@ -234,7 +233,7 @@
     anywhere = pl.BlockSpec(memory_space=pl.ANY)
     out = pl.pallas_call(
         functools.partial(kernel, nz, ny),
-        out_shape=jax.ShapeDtypeStruct((1, cols), jnp.float32),
+        out_shape=pltpu.VMEM((1, cols), jnp.float32),
         in_specs=[anywhere] * 3,
         out_specs=pl.BlockSpec(memory_space=pltpu.VMEM),
         scratch_shapes=[

time: 40.7 us -> 39.1 us (0.961)
  Pallas kernels: 39.3 us -> 38.4 us
  local copies, waits for them, and re-layouts: 1.27 us -> 0.59 us
    pallas_call x1, Pallas kernels: 39.3 us -> 38.4 us  [on_device(): pl.pallas_call(functools.partial(kernel, nz, ny), out_shape=pltpu.VMEM((1...]
    dynamic_slice x1, local copies, waits for them, and re-layouts: 1.27 us -> 0.59 us  [on_device(): return lax.dynamic_slice_in_dim(out.reshape(-1), start, portion)]
where the time goes in v3:
time: 39.1 us; the launch traced here: 39 us
  Pallas kernels  38.4 us (98%)
  local copies, waits for them, and re-layouts  0.59 us (2%)
    pallas_call x1, Pallas kernels, on_device(): pl.pallas_call(functools.partial(kernel, nz, ny), out_shape=pltpu.VMEM((1...  38.4 us

profile of v3, /device:TPU:1, one launch (start us, length us, event | category | flops | bytes accessed | tf_op | source)
XLA Modules:
  0.0 39.0 jit_solution(2662926375280751910)
XLA Ops:
  0.0 38.4 %shard_map.37 = f32[1,128]{1,0:T(1,128)S(1)} custom-call(bf16[2,64,1024]{2,1,0:T(8,128)(2,1)} %stem_hbm.1, bf16[16,512,128]{2,1,0:T(8,128)(2,1)} %mid_hbm.1, bf16[8,1024,128]{2,1,0:T(8,128)(2,1)} %bitcast.3), custom_call_target="tpu_custom_call" | custom-call | tf_op jit(solution)/shard_map/pallas_call | solution.py:234
  38.4 0.6 %dynamic-slice_bitcast_fusion = f32[64]{0:T(128)} fusion(f32[1,128]{1,0:T(1,128)S(1)} %shard_map.37, s32[]{:T(128)S(6)} %select_n.3), kind=kLoop, calls=%fused_computation | loop fusion | bytes 516 | tf_op jit(solution)/shard_map/dynamic_slice | solution.py:265

commit v4 on v3

--- a/solution.py
+++ b/solution.py
@@ -23,7 +23,7 @@
     nz, ny,
     stem_hbm, mid_hbm, right_hbm, out_ref,
     stem_v, mid_v, right_v, rhs_v, lhs_v, mix_v, acc_v, send1, recv1, send2, recv2,
-    stem_sem, mid_sem, right_sem, gs_send, gs_recv, r_send, r_recv,
+    stem_sem, mid_sem, right_sem, gs_send, gs_recv, r_send, r_recv, z_sem,
 ):
     cut, y = lax.axis_index("cuts"), lax.axis_index("stem")
     core = lax.rem(cut, NCORE)
@@ -53,7 +53,7 @@
         for c in range(NCORE):
             if d or c:
                 signal((at(z, xs[d], cores[c]), y))
-    for d in range(1, nz):
+    for d in (1, nz - 1):
         signal((at(lax.rem(z + d, nz), x, core), y))
 
     blocks = stem_hbm.shape[0]
@@ -63,7 +63,7 @@
     load_stem.start()
     load_mid.start()
     load_right.start()
-    pl.semaphore_wait(barrier, (ny - 1) + (NX * NCORE - 1) + (nz - 1))
+    pl.semaphore_wait(barrier, (ny - 1) + (NX * NCORE - 1) + 2)
 
     rows = stem_hbm.shape[1]
     half = rows // 2
@@ -90,6 +90,23 @@
     ]
     for copy in arriving:
         copy.start()
+
+    rounds, reach = [], 1
+    while reach < nz // 2:
+        rounds.append((2 * len(rounds), reach))
+        reach += rounds[-1][1]
+
+    def announce(n):
+        at_sem, step = rounds[n]
+        for way, d in enumerate((step, nz - step)):
+            device = (at(lax.rem(z + d, nz), x, core), y)
+            pl.semaphore_signal(z_sem.at[at_sem + way], inc=1, device_id=device, device_id_type=MESH)
+
+    def heard(n):
+        for way in range(2):
+            pl.semaphore_wait(z_sem.at[rounds[n][0] + way], 1)
+
+    announce(0)
     arrived = [piece(down, 0), piece(up, 1), piece(down, 1), piece(up, 0), piece(far, 0), piece(far, 1)]
     shared = [push(6 + n, arrived[n], arrived[n], (other, y)) for n in range(6)]
 
@@ -124,9 +141,13 @@
 
     load_stem.wait()
     load_right.wait()
+    heard(0)
+    announce(1)
     contract(0, y, cores[0], start=True)
     contract(1, y, cores[1])
     share(0, 1, 2, 3)
+    heard(1)
+    announce(2)
     contract(0, down, cores[0])
     contract(1, up, cores[0])
     for n in (0, 2):
@@ -141,6 +162,7 @@
         shared[n].wait_recv()
     contract(1, far, cores[1])
 
+    heard(2)
     top, bottom = acc_v[0:rows], acc_v[rows:]
     turned = pltpu.roll(bottom, r, axis=1)
     lane = lax.broadcasted_iota(jnp.int32, turned.shape, 1)
@@ -255,6 +277,7 @@
             pltpu.SemaphoreType.DMA((12,)),
             pltpu.SemaphoreType.DMA((2,)),
             pltpu.SemaphoreType.DMA((2,)),
+            pltpu.SemaphoreType.REGULAR((2 * nz.bit_length(),)),
         ],
         compiler_params=pltpu.CompilerParams(
             collective_id=0, has_side_effects=True, vmem_limit_bytes=60 * 2**20

time: 39.1 us -> 36.8 us (0.941)
  Pallas kernels: 38.4 us -> 36.1 us
    pallas_call x1, Pallas kernels: 38.4 us -> 36.1 us  [on_device(): pl.pallas_call(functools.partial(kernel, nz, ny), out_shape=pltpu.VMEM((1...]
where the time goes in v4:
time: 36.8 us; the launch traced here: 36.7 us
  Pallas kernels  36.1 us (98%)
  local copies, waits for them, and re-layouts  0.59 us (2%)
    pallas_call x1, Pallas kernels, on_device(): pl.pallas_call(functools.partial(kernel, nz, ny), out_shape=pltpu.VMEM((1...  36.1 us

profile of v4, /device:TPU:1, one launch (start us, length us, event | category | flops | bytes accessed | tf_op | source)
XLA Modules:
  0.0 36.7 jit_solution(12618816388128226885)
XLA Ops:
  0.0 36.1 %shard_map.37 = f32[1,128]{1,0:T(1,128)S(1)} custom-call(bf16[2,64,1024]{2,1,0:T(8,128)(2,1)} %stem_hbm.1, bf16[16,512,128]{2,1,0:T(8,128)(2,1)} %mid_hbm.1, bf16[8,1024,128]{2,1,0:T(8,128)(2,1)} %bitcast.3), custom_call_target="tpu_custom_call" | custom-call | tf_op jit(solution)/shard_map/pallas_call | solution.py:256
  36.1 0.6 %dynamic-slice_bitcast_fusion = f32[64]{0:T(128)} fusion(f32[1,128]{1,0:T(1,128)S(1)} %shard_map.37, s32[]{:T(128)S(6)} %select_n.3), kind=kLoop, calls=%fused_computation | loop fusion | bytes 516 | tf_op jit(solution)/shard_map/dynamic_slice | solution.py:288

commit v5 on v4

--- a/solution.py
+++ b/solution.py
@@ -46,6 +46,10 @@
     def at(z_, x_, core_):
         return (z_ * NX + x_) * NCORE + core_
 
+    blocks = stem_hbm.shape[0]
+    load_stem = pltpu.make_async_copy(stem_hbm, stem_v.at[pl.ds(y * blocks, blocks)], stem_sem)
+    load_stem.start()
+
     barrier = pltpu.get_barrier_semaphore()
     for d in range(1, ny):
         signal((cut, ys[d]))
@@ -53,17 +57,14 @@
         for c in range(NCORE):
             if d or c:
                 signal((at(z, xs[d], cores[c]), y))
-    for d in (1, nz - 1):
+    for d in (1, 2, nz - 2, nz - 1):
         signal((at(lax.rem(z + d, nz), x, core), y))
 
-    blocks = stem_hbm.shape[0]
-    load_stem = pltpu.make_async_copy(stem_hbm, stem_v.at[pl.ds(y * blocks, blocks)], stem_sem)
     load_mid = pltpu.make_async_copy(mid_hbm, mid_v, mid_sem)
     load_right = pltpu.make_async_copy(right_hbm, right_v, right_sem)
-    load_stem.start()
     load_mid.start()
     load_right.start()
-    pl.semaphore_wait(barrier, (ny - 1) + (NX * NCORE - 1) + 2)
+    pl.semaphore_wait(barrier, (ny - 1) + (NX * NCORE - 1) + 4)
 
     rows = stem_hbm.shape[1]
     half = rows // 2
@@ -79,19 +80,20 @@
             device_id=device, device_id_type=MESH,
         )
 
-    mine = [stem_hbm.at[core, pl.ds(h * half, half)] for h in (0, 1)]
+    load_stem.wait()
+    mine = [piece(y, 0), piece(y, 1)]
     arriving = [
         push(0, mine[0], piece(y, 0), (cut, up)),
         push(1, mine[1], piece(y, 1), (cut, down)),
         push(2, mine[1], piece(y, 1), (cut, up)),
         push(3, mine[0], piece(y, 0), (cut, down)),
-        push(4, mine[0], piece(y, 0), (cut, far)),
-        push(5, mine[1], piece(y, 1), (cut, far)),
+        push(4, piece(down, 0), piece(down, 0), (cut, up)),
+        push(5, piece(up, 1), piece(up, 1), (cut, down)),
     ]
-    for copy in arriving:
+    for copy in arriving[:4]:
         copy.start()
 
-    rounds, reach = [], 1
+    rounds, reach = [], 2
     while reach < nz // 2:
         rounds.append((2 * len(rounds), reach))
         reach += rounds[-1][1]
@@ -109,6 +111,10 @@
     announce(0)
     arrived = [piece(down, 0), piece(up, 1), piece(down, 1), piece(up, 0), piece(far, 0), piece(far, 1)]
     shared = [push(6 + n, arrived[n], arrived[n], (other, y)) for n in range(6)]
+
+    def pass_on(n):
+        arriving[n].wait_recv()
+        arriving[4 + n].start()
 
     def share(*which):
         for n in which:
@@ -139,40 +145,35 @@
         update = jnp.dot(mix_v[slot], right_v[y_ * blocks + core_], preferred_element_type=jnp.float32)
         acc_v[...] = update if start else acc_v[...] + update
 
-    load_stem.wait()
     load_right.wait()
+    contract(0, y, cores[0], start=True)
     heard(0)
     announce(1)
-    contract(0, y, cores[0], start=True)
     contract(1, y, cores[1])
-    share(0, 1, 2, 3)
-    heard(1)
-    announce(2)
+    pass_on(0)
+    pass_on(1)
+    for n in (0, 1):
+        shared[n].start()
+    share(2, 3)
     contract(0, down, cores[0])
     contract(1, up, cores[0])
     for n in (0, 2):
         shared[n].wait_recv()
     contract(0, down, cores[1])
-    share(4, 5)
-    contract(1, far, cores[0])
     for n in (1, 3):
         shared[n].wait_recv()
-    contract(0, up, cores[1])
+    contract(1, up, cores[1])
+    share(4, 5)
+    contract(0, far, cores[0])
     for n in (4, 5):
         shared[n].wait_recv()
     contract(1, far, cores[1])
 
-    heard(2)
+    heard(1)
     top, bottom = acc_v[0:rows], acc_v[rows:]
     turned = pltpu.roll(bottom, r, axis=1)
     lane = lax.broadcasted_iota(jnp.int32, turned.shape, 1)
     total = top + jnp.where(lane < r, -turned, turned)
-    for part_ in range(parts):
-        for x_ in range(NX):
-            for k in range(per):
-                row = (part_ * per + k) * NX + x_
-                send1[part_ * NX + x_, k:k + 1, :] = total[row:row + 1]
-
     place = x * parts + part
 
     def send(part_, x_):
@@ -183,6 +184,10 @@
         ).start()
 
     for part_ in range(parts):
+        for x_ in range(NX):
+            for k in range(per):
+                row = (part_ * per + k) * NX + x_
+                send1[part_ * NX + x_, k:k + 1, :] = total[row:row + 1]
         for x_ in range(NX):
             pl.when(place != x_ * parts + part_)(functools.partial(send, part_, x_))
     recv1[place] = send1[part * NX + x]

time: 36.8 us -> 36.1 us (0.981)
  Pallas kernels: 36.1 us -> 35.4 us
    pallas_call x1, Pallas kernels: 36.1 us -> 35.4 us  [on_device(): pl.pallas_call(functools.partial(kernel, nz, ny), out_shape=pltpu.VMEM((1...]
where the time goes in v5:
time: 36.1 us; the launch traced here: 36 us
  Pallas kernels  35.4 us (98%)
  local copies, waits for them, and re-layouts  0.59 us (2%)
    pallas_call x1, Pallas kernels, on_device(): pl.pallas_call(functools.partial(kernel, nz, ny), out_shape=pltpu.VMEM((1...  35.4 us

profile of v5, /device:TPU:1, one launch (start us, length us, event | category | flops | bytes accessed | tf_op | source)
XLA Modules:
  0.0 36.0 jit_solution(3109259630153782850)
XLA Ops:
  0.0 35.4 %shard_map.37 = f32[1,128]{1,0:T(1,128)S(1)} custom-call(bf16[2,64,1024]{2,1,0:T(8,128)(2,1)} %stem_hbm.1, bf16[16,512,128]{2,1,0:T(8,128)(2,1)} %mid_hbm.1, bf16[8,1024,128]{2,1,0:T(8,128)(2,1)} %bitcast.3), custom_call_target="tpu_custom_call" | custom-call | tf_op jit(solution)/shard_map/pallas_call | solution.py:261
  35.4 0.6 %dynamic-slice_bitcast_fusion = f32[64]{0:T(128)} fusion(f32[1,128]{1,0:T(1,128)S(1)} %shard_map.37, s32[]{:T(128)S(6)} %select_n.3), kind=kLoop, calls=%fused_computation | loop fusion | bytes 516 | tf_op jit(solution)/shard_map/dynamic_slice | solution.py:293

commit v6 on v5

--- a/solution.py
+++ b/solution.py
@@ -23,7 +23,7 @@
     nz, ny,
     stem_hbm, mid_hbm, right_hbm, out_ref,
     stem_v, mid_v, right_v, rhs_v, lhs_v, mix_v, acc_v, send1, recv1, send2, recv2,
-    stem_sem, mid_sem, right_sem, gs_send, gs_recv, r_send, r_recv, z_sem,
+    stem_sem, mid_sem, right_sem, gs_send, gs_recv, r_send, r_recv, round_sem,
 ):
     cut, y = lax.axis_index("cuts"), lax.axis_index("stem")
     core = lax.rem(cut, NCORE)
@@ -51,20 +51,33 @@
     load_stem.start()
 
     barrier = pltpu.get_barrier_semaphore()
-    for d in range(1, ny):
-        signal((cut, ys[d]))
-    for d in range(NX):
-        for c in range(NCORE):
-            if d or c:
-                signal((at(z, xs[d], cores[c]), y))
-    for d in (1, 2, nz - 2, nz - 1):
-        signal((at(lax.rem(z + d, nz), x, core), y))
+
+    def zs(d):
+        return (at(lax.rem(z + d, nz), x, core), y)
+
+    near = [(cut, ys[1]), (cut, ys[ny - 1]), (at(z, x, cores[1]), y)]
+    near += [(at(z, xs[d], core), y) for d in (1, NX - 1)] + [zs(d) for d in (1, nz - 1)]
+    for device in near:
+        signal(device)
+
+    rounds = [
+        near,
+        [(at(z, xs[2], core), y), (cut, ys[2]), zs(2), zs(nz - 2)],
+        [(at(z, x, cores[1]), y), zs(4), zs(nz - 4)],
+    ]
+
+    def announce(n):
+        for device in rounds[n]:
+            pl.semaphore_signal(round_sem.at[n], inc=1, device_id=device, device_id_type=MESH)
+
+    def heard(n):
+        pl.semaphore_wait(round_sem.at[n], len(rounds[n]))
 
     load_mid = pltpu.make_async_copy(mid_hbm, mid_v, mid_sem)
     load_right = pltpu.make_async_copy(right_hbm, right_v, right_sem)
     load_mid.start()
     load_right.start()
-    pl.semaphore_wait(barrier, (ny - 1) + (NX * NCORE - 1) + 4)
+    pl.semaphore_wait(barrier, len(near))
 
     rows = stem_hbm.shape[1]
     half = rows // 2
@@ -92,21 +105,6 @@
     ]
     for copy in arriving[:4]:
         copy.start()
-
-    rounds, reach = [], 2
-    while reach < nz // 2:
-        rounds.append((2 * len(rounds), reach))
-        reach += rounds[-1][1]
-
-    def announce(n):
-        at_sem, step = rounds[n]
-        for way, d in enumerate((step, nz - step)):
-            device = (at(lax.rem(z + d, nz), x, core), y)
-            pl.semaphore_signal(z_sem.at[at_sem + way], inc=1, device_id=device, device_id_type=MESH)
-
-    def heard(n):
-        for way in range(2):
-            pl.semaphore_wait(z_sem.at[rounds[n][0] + way], 1)
 
     announce(0)
     arrived = [piece(down, 0), piece(up, 1), piece(down, 1), piece(up, 0), piece(far, 0), piece(far, 1)]
@@ -146,12 +144,14 @@
         acc_v[...] = update if start else acc_v[...] + update
 
     load_right.wait()
-    contract(0, y, cores[0], start=True)
     heard(0)
     announce(1)
+    contract(0, y, cores[0], start=True)
     contract(1, y, cores[1])
     pass_on(0)
     pass_on(1)
+    heard(1)
+    announce(2)
     for n in (0, 1):
         shared[n].start()
     share(2, 3)
@@ -169,7 +169,7 @@
         shared[n].wait_recv()
     contract(1, far, cores[1])
 
-    heard(1)
+    heard(2)
     top, bottom = acc_v[0:rows], acc_v[rows:]
     turned = pltpu.roll(bottom, r, axis=1)
     lane = lax.broadcasted_iota(jnp.int32, turned.shape, 1)
@@ -282,7 +282,7 @@
             pltpu.SemaphoreType.DMA((12,)),
             pltpu.SemaphoreType.DMA((2,)),
             pltpu.SemaphoreType.DMA((2,)),
-            pltpu.SemaphoreType.REGULAR((2 * nz.bit_length(),)),
+            pltpu.SemaphoreType.REGULAR((3,)),
         ],
         compiler_params=pltpu.CompilerParams(
             collective_id=0, has_side_effects=True, vmem_limit_bytes=60 * 2**20

time: 36.1 us -> 35.6 us (0.986)
  Pallas kernels: 35.4 us -> 34.9 us
    pallas_call x1, Pallas kernels: 35.4 us -> 34.9 us  [on_device(): pl.pallas_call(functools.partial(kernel, nz, ny), out_shape=pltpu.VMEM((1...]
where the time goes in v6:
time: 35.6 us; the launch traced here: 35.5 us
  Pallas kernels  34.9 us (98%)
  local copies, waits for them, and re-layouts  0.59 us (2%)
    pallas_call x1, Pallas kernels, on_device(): pl.pallas_call(functools.partial(kernel, nz, ny), out_shape=pltpu.VMEM((1...  34.9 us

profile of v6, /device:TPU:1, one launch (start us, length us, event | category | flops | bytes accessed | tf_op | source)
XLA Modules:
  0.0 35.5 jit_solution(9245309818938304058)
XLA Ops:
  0.0 34.9 %shard_map.37 = f32[1,128]{1,0:T(1,128)S(1)} custom-call(bf16[2,64,1024]{2,1,0:T(8,128)(2,1)} %stem_hbm.1, bf16[16,512,128]{2,1,0:T(8,128)(2,1)} %mid_hbm.1, bf16[8,1024,128]{2,1,0:T(8,128)(2,1)} %bitcast.3), custom_call_target="tpu_custom_call" | custom-call | tf_op jit(solution)/shard_map/pallas_call | solution.py:261
  34.9 0.6 %dynamic-slice_bitcast_fusion = f32[64]{0:T(128)} fusion(f32[1,128]{1,0:T(1,128)S(1)} %shard_map.37, s32[]{:T(128)S(6)} %select_n.3), kind=kLoop, calls=%fused_computation | loop fusion | bytes 516 | tf_op jit(solution)/shard_map/dynamic_slice | solution.py:293

commit v7 on v6

--- a/solution.py
+++ b/solution.py
@@ -140,20 +140,21 @@
             mix_v[slot, :, n * tile:(n + 1) * tile] = jnp.dot(
                 lhs_v[slot], rhs_v[:, n * tile:(n + 1) * tile], preferred_element_type=jnp.float32
             ).astype(jnp.bfloat16)
+        if start:
+            load_right.wait()
         update = jnp.dot(mix_v[slot], right_v[y_ * blocks + core_], preferred_element_type=jnp.float32)
         acc_v[...] = update if start else acc_v[...] + update
 
-    load_right.wait()
     heard(0)
     announce(1)
     contract(0, y, cores[0], start=True)
     contract(1, y, cores[1])
     pass_on(0)
     pass_on(1)
+    for n in (0, 1):
+        shared[n].start()
     heard(1)
     announce(2)
-    for n in (0, 1):
-        shared[n].start()
     share(2, 3)
     contract(0, down, cores[0])
     contract(1, up, cores[0])

time: 35.6 us -> 35.6 us (level)
  no operation moved by 1% of the time
where the time goes in v7:
time: 35.6 us; the launch traced here: 35.5 us
  Pallas kernels  34.9 us (98%)
  local copies, waits for them, and re-layouts  0.59 us (2%)
    pallas_call x1, Pallas kernels, on_device(): pl.pallas_call(functools.partial(kernel, nz, ny), out_shape=pltpu.VMEM((1...  34.9 us

profile of v7, /device:TPU:1, one launch (start us, length us, event | category | flops | bytes accessed | tf_op | source)
XLA Modules:
  0.0 35.5 jit_solution(11597475428714618706)
XLA Ops:
  0.0 34.9 %shard_map.37 = f32[1,128]{1,0:T(1,128)S(1)} custom-call(bf16[2,64,1024]{2,1,0:T(8,128)(2,1)} %stem_hbm.1, bf16[16,512,128]{2,1,0:T(8,128)(2,1)} %mid_hbm.1, bf16[8,1024,128]{2,1,0:T(8,128)(2,1)} %bitcast.3), custom_call_target="tpu_custom_call" | custom-call | tf_op jit(solution)/shard_map/pallas_call | solution.py:262
  34.9 0.6 %dynamic-slice_bitcast_fusion = f32[64]{0:T(128)} fusion(f32[1,128]{1,0:T(1,128)S(1)} %shard_map.37, s32[]{:T(128)S(6)} %select_n.3), kind=kLoop, calls=%fused_computation | loop fusion | bytes 516 | tf_op jit(solution)/shard_map/dynamic_slice | solution.py:294
